TPU v7x, 32 devices: a whole 2x2x4 slice. The times are simulated.
32 devices in a mesh: fsdp: 4 (over z), ctx: 4 (over y, x), tp: 2 (over core).
Axes of the slice: x: 2, y: 2, z: 4, core: 2. Of those that a mesh axis runs over, the one named last changes fastest.
Arguments:
- hidden_in: bfloat16 [16, 1024, 768], P('fsdp', 'ctx'), may hold values from -6 to 6
- lengths: int32 [16], P('fsdp'), may hold values from 256 to 1024, as said below
- out_grad: bfloat16 [16, 1024, 768], P('fsdp', 'ctx'), may hold values from -6 to 6
- w_qkv: bfloat16 [3, 768, 768], P(None, 'fsdp', 'tp'), may hold values from -0.21875 to 0.21875
- qv_bias: bfloat16 [2, 12, 64], P(None, 'tp', 'fsdp'), may hold values from -0.3125 to 0.3125
- w_out: bfloat16 [768, 768], P('tp', 'fsdp'), may hold values from -3.5 to 3.5
- out_biases: bfloat16 [2, 768], P(None, 'fsdp'), may hold values from -4 to 4
- norm_gains: bfloat16 [2, 768], P(None, 'fsdp'), may hold values from 0.25 to 1.75
- norm_biases: bfloat16 [2, 768], P(None, 'fsdp'), may hold values from -4 to 4
- w_in: bfloat16 [768, 3072], P(None, ('fsdp', 'tp')), may hold values from -0.21875 to 0.21875
- ffn_bias: bfloat16 [3072], P(('fsdp', 'tp')), may hold values from -6 to 6
- w_ffo: bfloat16 [3072, 768], P(('fsdp', 'tp')), may hold values from -0.109375 to 0.109375
Outputs:
- hidden_out: bfloat16 [16, 1024, 768], P('fsdp', 'ctx')
- hidden_grad: bfloat16 [16, 1024, 768], P('fsdp', 'ctx')
- grad_qkv: float32 [3, 768, 768], P(None, 'fsdp', 'tp')
- grad_qv_bias: float32 [2, 12, 64], P(None, 'tp', 'fsdp')
- grad_out: float32 [768, 768], P('tp', 'fsdp')
- grad_out_biases: float32 [2, 768], P(None, 'fsdp')
- grad_gains: float32 [2, 768], P(None, 'fsdp')
- grad_shifts: float32 [2, 768], P(None, 'fsdp')
- grad_in: float32 [768, 3072], P(None, ('fsdp', 'tp'))
- grad_ffn_bias: float32 [3072], P(('fsdp', 'tp'))
- grad_ffo: float32 [3072, 768], P(('fsdp', 'tp'))
Inputs may be any that keep to these rules, and one draw needn't show every extreme that they name: lengths[s] counts the valid positions of slot s from its start; in every draw one slot has 1024 and one has 256.
All inputs are finite; a program needn't handle non-finite values.
Results may differ from a plain program's by a relative error of at most 0.019.
Values may be sent and summed in bfloat16 or wider, within the bound.
A program may use at most 192 MiB of HBM per device.

v0:
```python
import jax
import jax.numpy as jnp
from jax import lax
from jax.sharding import PartitionSpec as P

epsilon = 1e-05
masked_value = -1e30
heads_together = 2


def norm_rows(residual, gain_row, shift_row):
    centre = jnp.mean(residual, axis=-1, keepdims=True)
    centred = residual - centre
    spread = jnp.mean(centred * centred, axis=-1, keepdims=True)
    return centred * lax.rsqrt(spread + epsilon) * gain_row + shift_row


def gelu_exact(values):
    return jax.nn.gelu(values, approximate=False)


def split_heads(matrix, head_dim):
    return matrix.reshape(matrix.shape[0], matrix.shape[1] // head_dim, head_dim)


def block_scores(query_heads, key_heads, key_mask, score_scale):
    scores = (
        jnp.einsum("qhd,khd->hqk", query_heads, key_heads, preferred_element_type=jnp.float32)
        * score_scale
    )
    return jnp.where(key_mask[None, None, :], scores, masked_value)


def attend_slot(queries, key_value, length, score_scale, head_dim):
    gathered = lax.all_gather(key_value, "ctx", axis=1, tiled=True)
    seq_len = gathered.shape[1]
    key_mask = lax.iota(jnp.int32, seq_len) < length
    block_width = heads_together * head_dim
    outputs = []
    totals = []
    for head_block in range(queries.shape[1] // block_width):
        columns = slice(head_block * block_width, (head_block + 1) * block_width)
        query_heads = split_heads(queries[:, columns], head_dim)
        key_heads = split_heads(gathered[0][:, columns], head_dim)
        value_heads = split_heads(gathered[1][:, columns], head_dim)
        scores = block_scores(query_heads, key_heads, key_mask, score_scale)
        highest = jnp.max(scores, axis=-1, keepdims=True)
        log_total = highest + jnp.log(jnp.sum(jnp.exp(scores - highest), axis=-1, keepdims=True))
        weights_low = jnp.exp(scores - log_total).astype(jnp.bfloat16)
        attended = jnp.einsum(
            "hqk,khd->qhd", weights_low, value_heads, preferred_element_type=jnp.float32
        )
        outputs.append(attended.reshape(attended.shape[0], block_width))
        totals.append(log_total[:, :, 0])
    return (jnp.concatenate(outputs, axis=1).astype(jnp.bfloat16), jnp.concatenate(totals, axis=0))


def slot_grads(queries, key_value, length, grad_mixed, log_totals, score_scale, head_dim):
    gathered = lax.all_gather(key_value, "ctx", axis=1, tiled=True)
    seq_len = gathered.shape[1]
    key_mask = lax.iota(jnp.int32, seq_len) < length
    block_width = heads_together * head_dim
    query_grads = []
    key_grads = []
    value_grads = []
    inner_parts = []
    for head_block in range(queries.shape[1] // block_width):
        columns = slice(head_block * block_width, (head_block + 1) * block_width)
        heads_range = slice(head_block * heads_together, (head_block + 1) * heads_together)
        query_heads = split_heads(queries[:, columns], head_dim)
        key_heads = split_heads(gathered[0][:, columns], head_dim)
        value_heads = split_heads(gathered[1][:, columns], head_dim)
        grad_heads = split_heads(grad_mixed[:, columns], head_dim)
        scores = block_scores(query_heads, key_heads, key_mask, score_scale)
        softmax_rows = jnp.exp(scores - log_totals[heads_range, :, None])
        grad_weights = jnp.einsum(
            "qhd,khd->hqk", grad_heads, value_heads, preferred_element_type=jnp.float32
        )
        inner_sums = jnp.sum(softmax_rows * grad_weights, axis=-1)
        grad_scores = (softmax_rows * (grad_weights - inner_sums[:, :, None])).astype(jnp.bfloat16)
        grad_query = (
            jnp.einsum("hqk,khd->qhd", grad_scores, key_heads, preferred_element_type=jnp.float32)
            * score_scale
        )
        query_grads.append(grad_query.reshape(grad_query.shape[0], block_width))
        inner_parts.append(inner_sums)
        grad_key = (
            jnp.einsum("hqk,qhd->khd", grad_scores, query_heads, preferred_element_type=jnp.float32)
            * score_scale
        )
        grad_value = jnp.einsum(
            "hqk,qhd->khd",
            softmax_rows.astype(jnp.bfloat16),
            grad_heads,
            preferred_element_type=jnp.float32,
        )
        key_grads.append(grad_key.reshape(seq_len, block_width))
        value_grads.append(grad_value.reshape(seq_len, block_width))
    grad_queries = jnp.concatenate(query_grads, axis=1)
    key_terms = jnp.stack(
        [jnp.concatenate(key_grads, axis=1), jnp.concatenate(value_grads, axis=1)]
    )
    own_grads = lax.psum_scatter(
        key_terms.astype(jnp.bfloat16), "ctx", scatter_dimension=1, tiled=True
    ).astype(jnp.float32)
    return (grad_queries, own_grads)


def per_device(
    hidden_in,
    lengths,
    out_grad,
    w_qkv,
    qv_bias,
    w_out,
    out_biases,
    norm_gains,
    norm_biases,
    w_in,
    ffn_bias,
    w_ffo,
):
    w_proj, proj_bias, w_back, branch_biases, gains, shifts, w_up, up_bias, w_down = (
        lax.all_gather(w_qkv, "fsdp", axis=1, tiled=True),
        lax.all_gather(qv_bias, "fsdp", axis=2, tiled=True),
        lax.all_gather(w_out, "fsdp", axis=1, tiled=True),
        lax.all_gather(out_biases, "fsdp", axis=1, tiled=True),
        lax.all_gather(norm_gains, "fsdp", axis=1, tiled=True),
        lax.all_gather(norm_biases, "fsdp", axis=1, tiled=True),
        lax.all_gather(w_in, "fsdp", axis=1, tiled=True),
        lax.all_gather(ffn_bias, "fsdp", axis=0, tiled=True),
        lax.all_gather(w_ffo, "fsdp", axis=0, tiled=True),
    )
    slot_count, block_len, model_width = hidden_in.shape
    token_count = slot_count * block_len
    head_dim = proj_bias.shape[2]
    score_scale = head_dim ** (-0.5)
    local_width = w_proj.shape[2]
    contract_rows = (((0,), (0,)), ((), ()))
    contract_cols = (((1,), (1,)), ((), ()))
    bias_table = jnp.stack(
        [
            proj_bias[0].reshape(local_width).astype(jnp.float32),
            jnp.zeros((local_width,), jnp.float32),
            proj_bias[1].reshape(local_width).astype(jnp.float32),
        ]
    )
    projected = (
        jnp.einsum("sbd,pdc->spbc", hidden_in, w_proj, preferred_element_type=jnp.float32)
        + bias_table[None, :, None, :]
    ).astype(jnp.bfloat16)
    queries = projected[:, 0]
    key_values = projected[:, 1:]
    attended, log_totals = lax.map(
        lambda slot_items: attend_slot(
            slot_items[0], slot_items[1], slot_items[2], score_scale, head_dim
        ),
        (queries, key_values, lengths),
    )
    mixed_rows = attended.reshape(token_count, local_width)
    token_rows = hidden_in.reshape(token_count, model_width)
    branch = lax.psum(
        jnp.dot(mixed_rows, w_back, preferred_element_type=jnp.float32), "tp"
    ) + branch_biases[0].astype(jnp.float32)
    first_norm, first_pull = jax.vjp(
        norm_rows,
        token_rows.astype(jnp.float32) + branch,
        gains[0].astype(jnp.float32),
        shifts[0].astype(jnp.float32),
    )
    first_low = first_norm.astype(jnp.bfloat16)
    hidden_pre = jnp.dot(first_low, w_up, preferred_element_type=jnp.float32) + up_bias.astype(
        jnp.float32
    )
    activated, gelu_pull = jax.vjp(gelu_exact, hidden_pre)
    activated_low = activated.astype(jnp.bfloat16)
    second_branch = lax.psum(
        jnp.dot(activated_low, w_down, preferred_element_type=jnp.float32), "tp"
    ) + branch_biases[1].astype(jnp.float32)
    output_rows, second_pull = jax.vjp(
        norm_rows,
        first_norm + second_branch,
        gains[1].astype(jnp.float32),
        shifts[1].astype(jnp.float32),
    )
    hidden_out = output_rows.astype(jnp.bfloat16).reshape(slot_count, block_len, model_width)
    own_start = lax.axis_index("ctx") * block_len
    positions = own_start + lax.iota(jnp.int32, block_len)
    row_mask = (positions[None, :] < lengths[:, None]).astype(jnp.float32).reshape(token_count, 1)
    grad_output = out_grad.reshape(token_count, model_width).astype(jnp.float32) * row_mask
    grad_second, grad_gain_two, grad_shift_two = second_pull(grad_output)
    grad_second_low = grad_second.astype(jnp.bfloat16)
    grad_down = lax.dot_general(
        activated_low, grad_second_low, contract_rows, preferred_element_type=jnp.float32
    )
    grad_act = lax.dot_general(
        grad_second_low, w_down, contract_cols, preferred_element_type=jnp.float32
    )
    (grad_pre,) = gelu_pull(grad_act)
    grad_pre_low = grad_pre.astype(jnp.bfloat16)
    grad_up = lax.dot_general(
        first_low, grad_pre_low, contract_rows, preferred_element_type=jnp.float32
    )
    grad_first = grad_second + lax.psum(
        lax.dot_general(grad_pre_low, w_up, contract_cols, preferred_element_type=jnp.float32), "tp"
    )
    grad_resid, grad_gain_one, grad_shift_one = first_pull(grad_first)
    grad_branch_low = grad_resid.astype(jnp.bfloat16)
    grad_back = lax.dot_general(
        mixed_rows, grad_branch_low, contract_rows, preferred_element_type=jnp.float32
    )
    grad_mixed = (
        lax.dot_general(grad_branch_low, w_back, contract_cols, preferred_element_type=jnp.float32)
        .astype(jnp.bfloat16)
        .reshape(slot_count, block_len, local_width)
    )
    grad_queries, grad_pairs = lax.map(
        lambda slot_items: slot_grads(
            slot_items[0],
            slot_items[1],
            slot_items[2],
            slot_items[3],
            slot_items[4],
            score_scale,
            head_dim,
        ),
        (queries, key_values, lengths, grad_mixed, log_totals),
    )
    grad_proj = jnp.concatenate(
        [grad_queries.astype(jnp.bfloat16)[:, None], grad_pairs.astype(jnp.bfloat16)], axis=1
    )
    grad_w_proj = jnp.einsum(
        "sbd,spbc->pdc", hidden_in, grad_proj, preferred_element_type=jnp.float32
    )
    grad_proj_bias = jnp.stack(
        [
            jnp.sum(grad_proj[:, 0], axis=(0, 1), dtype=jnp.float32),
            jnp.sum(grad_proj[:, 2], axis=(0, 1), dtype=jnp.float32),
        ]
    ).reshape(proj_bias.shape)
    grad_tokens = jnp.einsum(
        "spbc,pdc->sbd", grad_proj, w_proj, preferred_element_type=jnp.float32
    ).reshape(token_count, model_width)
    hidden_grad = (
        (grad_resid + lax.psum(grad_tokens.astype(jnp.bfloat16), "tp").astype(jnp.float32))
        .astype(jnp.bfloat16)
        .reshape(slot_count, block_len, model_width)
    )
    grad_biases = jnp.stack(
        [
            jnp.sum(grad_branch_low, axis=0, dtype=jnp.float32),
            jnp.sum(grad_second_low, axis=0, dtype=jnp.float32),
        ]
    )
    grad_gains = jnp.stack([grad_gain_one, grad_gain_two])
    grad_shifts = jnp.stack([grad_shift_one, grad_shift_two])
    grad_up_bias = jnp.sum(grad_pre_low, axis=0, dtype=jnp.float32)
    shares = (
        lax.psum_scatter(
            grad_w_proj.astype(jnp.bfloat16), "fsdp", scatter_dimension=1, tiled=True
        ).astype(jnp.float32),
        lax.psum_scatter(
            grad_proj_bias.astype(jnp.bfloat16), "fsdp", scatter_dimension=2, tiled=True
        ).astype(jnp.float32),
        lax.psum_scatter(
            grad_back.astype(jnp.bfloat16), "fsdp", scatter_dimension=1, tiled=True
        ).astype(jnp.float32),
        lax.psum_scatter(
            grad_biases.astype(jnp.bfloat16), "fsdp", scatter_dimension=1, tiled=True
        ).astype(jnp.float32),
        lax.psum_scatter(
            grad_gains.astype(jnp.bfloat16), "fsdp", scatter_dimension=1, tiled=True
        ).astype(jnp.float32),
        lax.psum_scatter(
            grad_shifts.astype(jnp.bfloat16), "fsdp", scatter_dimension=1, tiled=True
        ).astype(jnp.float32),
        lax.psum_scatter(
            grad_up.astype(jnp.bfloat16), "fsdp", scatter_dimension=1, tiled=True
        ).astype(jnp.float32),
        lax.psum_scatter(
            grad_up_bias.astype(jnp.bfloat16), "fsdp", scatter_dimension=0, tiled=True
        ).astype(jnp.float32),
        lax.psum_scatter(
            grad_down.astype(jnp.bfloat16), "fsdp", scatter_dimension=0, tiled=True
        ).astype(jnp.float32),
    )
    owned = (
        lax.psum(shares[0].astype(jnp.bfloat16), "ctx").astype(jnp.float32),
        lax.psum(shares[1].astype(jnp.bfloat16), "ctx").astype(jnp.float32),
        lax.psum(shares[2].astype(jnp.bfloat16), "ctx").astype(jnp.float32),
        lax.psum(shares[3].astype(jnp.bfloat16), "ctx").astype(jnp.float32),
        lax.psum(shares[4].astype(jnp.bfloat16), "ctx").astype(jnp.float32),
        lax.psum(shares[5].astype(jnp.bfloat16), "ctx").astype(jnp.float32),
        lax.psum(shares[6].astype(jnp.bfloat16), "ctx").astype(jnp.float32),
        lax.psum(shares[7].astype(jnp.bfloat16), "ctx").astype(jnp.float32),
        lax.psum(shares[8].astype(jnp.bfloat16), "ctx").astype(jnp.float32),
    )
    return (
        hidden_out,
        hidden_grad,
        owned[0],
        owned[1],
        owned[2],
        owned[3],
        owned[4],
        owned[5],
        owned[6],
        owned[7],
        owned[8],
    )


def solution(mesh):
    return jax.shard_map(
        per_device,
        mesh=mesh,
        in_specs=(
            P("fsdp", "ctx", None),
            P("fsdp"),
            P("fsdp", "ctx", None),
            P(None, "fsdp", "tp"),
            P(None, "tp", "fsdp"),
            P("tp", "fsdp"),
            P(None, "fsdp"),
            P(None, "fsdp"),
            P(None, "fsdp"),
            P(None, ("fsdp", "tp")),
            P(("fsdp", "tp")),
            P(("fsdp", "tp"), None),
        ),
        out_specs=(
            P("fsdp", "ctx", None),
            P("fsdp", "ctx", None),
            P(None, "fsdp", "tp"),
            P(None, "tp", "fsdp"),
            P("tp", "fsdp"),
            P(None, "fsdp"),
            P(None, "fsdp"),
            P(None, "fsdp"),
            P(None, ("fsdp", "tp")),
            P(("fsdp", "tp")),
            P(("fsdp", "tp"), None),
        ),
        check_vma=False,
    )
```

profile of v0, /device:TPU:0, one launch (start us, length us, event | category | flops | bytes accessed | tf_op | source)
XLA Modules:
  0.0 1103.6 jit_solution(3920871484078852565)
XLA Ops:
  8.7 14.8 %all_gather.34 = bf16[2,6,64]{1,0,2:T(2,128)(2,1)S(1)} all-gather(bf16[2,6,16]{1,0,2:T(2,128)(2,1)S(1)} %copy.57), channel_id=1, replica_groups=mesh['fsdp'=4,'ctx'=4,'tp'=2] {'fsdp'}, dimensions={2}, use_global_device_ids=true | all-gather | bytes 1920 | tf_op jit(solution)/shard_map/all_gather | solution.py:125
  24.0 24.4 %all_gather.35 = bf16[384,768]{0,1:T(8,128)(2,1)S(1)} all-gather(bf16[384,192]{0,1:T(8,128)(2,1)} %param.21), channel_id=1, replica_groups=mesh['fsdp'=4,'ctx'=4,'tp'=2] {'fsdp'}, dimensions={1}, use_global_device_ids=true | all-gather | bytes 737280 | tf_op jit(solution)/shard_map/all_gather | solution.py:126
  48.5 13.6 %all-gather.16.cloned.1.call-done = bf16[3,768,384]{2,1,0:T(8,128)(2,1)} async-done(((bf16[3,192,384]{2,1,0:T(8,128)(2,1)}), bf16[3,768,384]{2,1,0:T(8,128)(2,1)}) %all-gather.16.cloned.1.call-update) | async-done | bytes 1769488 | tf_op jit(solution)/shard_map/all_gather | solution.py:124
  67.7 162.6 %while.24 = (s32[]{:T(128)}, bf16[4,256,384]{2,1,0:T(8,128)(2,1)S(1)}, f32[4,6,256]{2,1,0:T(8,128)S(1)}, bf16[4,2,256,384]{2,3,1,0:T(8,128)(2,1)}, s32[4]{0:T(12...) while((s32[]{:T(128)}, bf16[4,256,384]{2,1,0:T(8,128)(2,1)S(1)}, f32[4,6,256]{2,1,0:T(8,128)S(1)}, ...), condition=%wide.region_7.8_spmd, body=%wide.region_0.7_spmd.sunk | while | flops 414353920 | bytes 35844252 | solution.py:154
  70.8 30.0 %all-gather.22.cloned.1.call-done = bf16[1,2,1024,384]{2,3,1,0:T(8,128)(2,1)} async-done(((bf16[1,2,256,384]{2,3,1,0:T(8,128)(2,1)}), bf16[1,2,1024,384]{2,3,1,0:T(8,128)(2,1)}) %all-gather.22.cloned.1.call-update) | async-done | bytes 1572880 | tf_op jit(solution)/shard_map/while/body/eval_jaxpr/all_gather | solution.py:35
  110.8 31.1 %all-gather.22.cloned.1.call-done = bf16[1,2,1024,384]{2,3,1,0:T(8,128)(2,1)} async-done(((bf16[1,2,256,384]{2,3,1,0:T(8,128)(2,1)}), bf16[1,2,1024,384]{2,3,1,0:T(8,128)(2,1)}) %all-gather.22.cloned.1.call-update) | async-done | bytes 1572880 | tf_op jit(solution)/shard_map/while/body/eval_jaxpr/all_gather | solution.py:35
  151.9 30.8 %all-gather.22.cloned.1.call-done = bf16[1,2,1024,384]{2,3,1,0:T(8,128)(2,1)} async-done(((bf16[1,2,256,384]{2,3,1,0:T(8,128)(2,1)}), bf16[1,2,1024,384]{2,3,1,0:T(8,128)(2,1)}) %all-gather.22.cloned.1.call-update) | async-done | bytes 1572880 | tf_op jit(solution)/shard_map/while/body/eval_jaxpr/all_gather | solution.py:35
  192.7 30.8 %all-gather.22.cloned.1.call-done = bf16[1,2,1024,384]{2,3,1,0:T(8,128)(2,1)} async-done(((bf16[1,2,256,384]{2,3,1,0:T(8,128)(2,1)}), bf16[1,2,1024,384]{2,3,1,0:T(8,128)(2,1)}) %all-gather.22.cloned.1.call-update) | async-done | bytes 1572880 | tf_op jit(solution)/shard_map/while/body/eval_jaxpr/all_gather | solution.py:35
  234.7 10.9 all-gather.2
  263.2 12.2 %all-gather.5 = bf16[4,1,384]{2,1,0:T(2,128)(2,1)S(1)} all-gather(bf16[1,1,384]{2,1,0:T(2,128)(2,1)S(1)} %reshape.402), channel_id=1, replica_groups=mesh['fsdp'=4,'ctx'=4,'tp'=2] {'fsdp'}, dimensions={0}, use_global_device_ids=true | all-gather | bytes 3840 | tf_op jit(solution)/shard_map/all_gather | solution.py:131
  278.9 30.8 %all-gather.18.cloned.1.call-done = bf16[768,1536]{1,0:T(8,128)(2,1)} async-done(((bf16[768,384]{1,0:T(8,128)(2,1)}), bf16[768,1536]{1,0:T(8,128)(2,1)}) %all-gather.18.cloned.1.call-update) | async-done | bytes 2359312 | tf_op jit(solution)/shard_map/all_gather | solution.py:130
  309.7 19.5 %multiply_convert_fusion.3 = (bf16[1024,1536]{1,0:T(8,128)(2,1)}, f32[1024,1536]{1,0:T(8,128)}, f32[1024,1536]{1,0:T(8,128)}) fusion(f32[1536]{0:T(1024)S(1)} %reshape.404, bf16[768,1536]{1,0:T(8,128)(2,1)} %all-gather.18.cloned.1.call-done, f32[1024,768]{1,0:T(8,128)S(1)} %get-tuple-element.255, f32[768]{0:T(1024)S(1)} %get-tuple-element.199, ...), kind=kOutput, calls=%fused_computation.70 | convolution fusion | flops 2523660288 | bytes 21254144 | tf_op jit(solution)/shard_map/dot_general | solution.py:172
  329.3 31.3 %all-gather.20.cloned.1.call-done = bf16[1536,768]{1,0:T(8,128)(2,1)} async-done(((bf16[384,768]{1,0:T(8,128)(2,1)}), bf16[1536,768]{1,0:T(8,128)(2,1)}) %all-gather.20.cloned.1.call-update) | async-done | bytes 2359312 | tf_op jit(solution)/shard_map/all_gather | solution.py:132
  368.7 21.0 %all-reduce.11.cloned.1.call-done = f32[1024,768]{1,0:T(8,128)} async-done(((f32[1024,768]{1,0:T(8,128)}), f32[1024,768]{1,0:T(8,128)}) %all-reduce.11.cloned.1.call-update) | async-done | bytes 3145744 | tf_op jit(solution)/shard_map/psum | solution.py:177
  422.6 14.0 %all-reduce.13.cloned.1.call-done = f32[1024,768]{1,0:T(8,128)} async-done(((f32[1024,768]{1,0:T(8,128)}), f32[1024,768]{1,0:T(8,128)}) %all-reduce.13.cloned.1.call-update) | async-done | bytes 3145744 | tf_op jit(solution)/shard_map/psum | solution.py:204
  444.3 306.6 %while.25 = (s32[]{:T(128)}, bf16[4,256,384]{2,1,0:T(8,128)(2,1)}, bf16[4,2,256,384]{3,2,1,0:T(8,128)(2,1)}, bf16[4,2,256,384]{2,3,1,0:T(8,128)(2,1)}, s32[4]{0:...) while((s32[]{:T(128)}, bf16[4,256,384]{2,1,0:T(8,128)(2,1)}, ...), condition=%wide.region_24.25_spmd, body=%wide.region_19.24_spmd.sunk | while | flops 1028259328 | bytes 90409344 | solution.py:217
  449.1 30.3 %all-gather.24.cloned.1.call-done = bf16[1,2,1024,384]{2,3,1,0:T(8,128)(2,1)} async-done(((bf16[1,2,256,384]{2,3,1,0:T(8,128)(2,1)}), bf16[1,2,1024,384]{2,3,1,0:T(8,128)(2,1)}) %all-gather.24.cloned.1.call-update) | async-done | bytes 1572880 | tf_op jit(solution)/shard_map/while/body/eval_jaxpr/all_gather | solution.py:59
  493.3 26.9 %reduce-scatter.38.cloned.1.call-done = bf16[2,256,384]{1,2,0:T(8,128)(2,1)} async-done(((bf16[2,1024,384]{1,2,0:T(8,128)(2,1)}), bf16[2,256,384]{1,2,0:T(8,128)(2,1)}) %reduce-scatter.38.cloned.1.call-update) | async-done | bytes 393232 | tf_op jit(solution)/shard_map/while/body/eval_jaxpr/reduce_scatter | solution.py:103
  526.7 29.1 %all-gather.24.cloned.1.call-done = bf16[1,2,1024,384]{2,3,1,0:T(8,128)(2,1)} async-done(((bf16[1,2,256,384]{2,3,1,0:T(8,128)(2,1)}), bf16[1,2,1024,384]{2,3,1,0:T(8,128)(2,1)}) %all-gather.24.cloned.1.call-update) | async-done | bytes 1572880 | tf_op jit(solution)/shard_map/while/body/eval_jaxpr/all_gather | solution.py:59
  569.7 26.9 %reduce-scatter.38.cloned.1.call-done = bf16[2,256,384]{1,2,0:T(8,128)(2,1)} async-done(((bf16[2,1024,384]{1,2,0:T(8,128)(2,1)}), bf16[2,256,384]{1,2,0:T(8,128)(2,1)}) %reduce-scatter.38.cloned.1.call-update) | async-done | bytes 393232 | tf_op jit(solution)/shard_map/while/body/eval_jaxpr/reduce_scatter | solution.py:103
  603.1 28.8 %all-gather.24.cloned.1.call-done = bf16[1,2,1024,384]{2,3,1,0:T(8,128)(2,1)} async-done(((bf16[1,2,256,384]{2,3,1,0:T(8,128)(2,1)}), bf16[1,2,1024,384]{2,3,1,0:T(8,128)(2,1)}) %all-gather.24.cloned.1.call-update) | async-done | bytes 1572880 | tf_op jit(solution)/shard_map/while/body/eval_jaxpr/all_gather | solution.py:59
  645.8 26.9 %reduce-scatter.38.cloned.1.call-done = bf16[2,256,384]{1,2,0:T(8,128)(2,1)} async-done(((bf16[2,1024,384]{1,2,0:T(8,128)(2,1)}), bf16[2,256,384]{1,2,0:T(8,128)(2,1)}) %reduce-scatter.38.cloned.1.call-update) | async-done | bytes 393232 | tf_op jit(solution)/shard_map/while/body/eval_jaxpr/reduce_scatter | solution.py:103
  679.3 28.8 %all-gather.24.cloned.1.call-done = bf16[1,2,1024,384]{2,3,1,0:T(8,128)(2,1)} async-done(((bf16[1,2,256,384]{2,3,1,0:T(8,128)(2,1)}), bf16[1,2,1024,384]{2,3,1,0:T(8,128)(2,1)}) %all-gather.24.cloned.1.call-update) | async-done | bytes 1572880 | tf_op jit(solution)/shard_map/while/body/eval_jaxpr/all_gather | solution.py:59
  721.9 26.9 %reduce-scatter.38.cloned.1.call-done = bf16[2,256,384]{1,2,0:T(8,128)(2,1)} async-done(((bf16[2,1024,384]{1,2,0:T(8,128)(2,1)}), bf16[2,256,384]{1,2,0:T(8,128)(2,1)}) %reduce-scatter.38.cloned.1.call-update) | async-done | bytes 393232 | tf_op jit(solution)/shard_map/while/body/eval_jaxpr/reduce_scatter | solution.py:103
  785.2 16.9 %reduce-scatter.36.cloned.1.call-done = bf16[384,768]{1,0:T(8,128)(2,1)} async-done(((bf16[1536,768]{1,0:T(8,128)(2,1)}), bf16[384,768]{1,0:T(8,128)(2,1)}) %reduce-scatter.36.cloned.1.call-update) | async-done | bytes 589840
  804.3 38.1 %reduce-scatter.26.cloned.1.call-done = bf16[192,1152]{1,0:T(8,128)(2,1)} async-done(((bf16[768,1152]{1,0:T(8,128)(2,1)}), bf16[192,1152]{1,0:T(8,128)(2,1)}) %reduce-scatter.26.cloned.1.call-update) | async-done | bytes 442384
  846.6 19.7 %reduce-scatter.22.cloned.1.call-done = bf16[384,192]{0,1:T(8,128)(2,1)} async-done(((bf16[384,768]{0,1:T(8,128)(2,1)}), bf16[384,192]{0,1:T(8,128)(2,1)}) %reduce-scatter.22.cloned.1.call-update) | async-done | bytes 147472 | tf_op jit(solution)/shard_map/reduce_scatter | solution.py:265
  866.3 48.7 %reduce-scatter.24.cloned.1.call-done = bf16[384,768]{1,0:T(8,128)(2,1)} async-done(((bf16[1536,768]{1,0:T(8,128)(2,1)}), bf16[384,768]{1,0:T(8,128)(2,1)}) %reduce-scatter.24.cloned.1.call-update) | async-done | bytes 589840 | tf_op jit(solution)/shard_map/reduce_scatter | solution.py:283
  936.6 18.9 %reduce-scatter.32.cloned.1.call-done = bf16[192,2]{1,0:T(8,128)(2,1)} async-done(((bf16[768,2]{1,0:T(8,128)(2,1)}), bf16[192,2]{1,0:T(8,128)(2,1)}) %reduce-scatter.32.cloned.1.call-update) | async-done | bytes 784
  956.3 19.6 %reduce-scatter.30.cloned.1.call-done = bf16[192,2]{1,0:T(8,128)(2,1)} async-done(((bf16[768,2]{1,0:T(8,128)(2,1)}), bf16[192,2]{1,0:T(8,128)(2,1)}) %reduce-scatter.30.cloned.1.call-update) | async-done | bytes 784
  976.8 18.9 %reduce-scatter.34.cloned.1.call-done = bf16[192,2]{1,0:T(8,128)(2,1)} async-done(((bf16[768,2]{1,0:T(8,128)(2,1)}), bf16[192,2]{1,0:T(8,128)(2,1)}) %reduce-scatter.34.cloned.1.call-update) | async-done | bytes 784
  1020.1 70.2 %all-reduce.17.cloned.1.call-done = (bf16[3,192,384]{1,2,0:T(8,128)(2,1)}, bf16[384,192]{0,1:T(8,128)(2,1)}, bf16[768,384]{1,0:T(8,128)(2,1)}, bf16[384,768]{1,0:T(8,128)(2,1)}) async-done(((bf16[3,192,384]{1,2,0:T(8,128)(2,1)}, bf16[384,192]{0,1:T(8,128)(2,1)}, bf16[768,384]{1,0:T(8,128)(2,1)}, bf16[384,768]{1,0:T(8,128)(2,1)}), (bf16[3,192,384]{1,2,0:T(8,128)(2,1)}, bf16[384,192]{0,1:T(8,128)(2,1)}, ...) | async-done | bytes 1769488 | tf_op jit(solution)/shard_map/psum | solution.py:288
  (501 shorter events, 295.3 us)
Async XLA Ops:
  7.2 54.9 %all-gather.16.cloned.1.call-start = ((), (), s32[]{:S(2)}) async-start(), calls=%async_computation.9 | async-start | bytes 2211840 | tf_op jit(solution)/shard_map/all_gather | solution.py:124
  48.4 182.0 %copy-start.8 = (bf16[384,768]{0,1:T(8,128)(2,1)}, bf16[384,768]{0,1:T(8,128)(2,1)S(1)}, u32[]{:S(2)}) copy-start(bf16[384,768]{0,1:T(8,128)(2,1)S(1)} %all_gather.35) | copy-start | bytes 1769476
  67.7 33.1 %all-gather.22.cloned.1.call-start = ((), (), s32[]{:S(2)}) async-start(), calls=%async_computation.25 | async-start | bytes 1966080 | tf_op jit(solution)/shard_map/while/body/eval_jaxpr/all_gather | solution.py:35
  107.7 34.3 %all-gather.22.cloned.1.call-start = ((), (), s32[]{:S(2)}) async-start(), calls=%async_computation.25 | async-start | bytes 1966080 | tf_op jit(solution)/shard_map/while/body/eval_jaxpr/all_gather | solution.py:35
  148.8 33.9 %all-gather.22.cloned.1.call-start = ((), (), s32[]{:S(2)}) async-start(), calls=%async_computation.25 | async-start | bytes 1966080 | tf_op jit(solution)/shard_map/while/body/eval_jaxpr/all_gather | solution.py:35
  189.5 33.9 %all-gather.22.cloned.1.call-start = ((), (), s32[]{:S(2)}) async-start(), calls=%async_computation.25 | async-start | bytes 1966080 | tf_op jit(solution)/shard_map/while/body/eval_jaxpr/all_gather | solution.py:35
  230.3 45.2 %all-reduce.9.cloned.1.call-start = ((), (), s32[]{:S(2)}) async-start(), calls=%async_computation.10 | async-start | bytes 6291456 | tf_op jit(solution)/shard_map/psum | solution.py:162
  233.2 76.5 %all-gather.18.cloned.1.call-start = ((), (), s32[]{:S(2)}) async-start(), calls=%async_computation.11 | async-start | bytes 2949120 | tf_op jit(solution)/shard_map/all_gather | solution.py:130
  233.9 126.7 %all-gather.20.cloned.1.call-start = ((), (), s32[]{:S(2)}) async-start(), calls=%async_computation.12 | async-start | bytes 2949120 | tf_op jit(solution)/shard_map/all_gather | solution.py:132
  234.7 155.0 %all-reduce.11.cloned.1.call-start = ((), (), s32[]{:S(2)}) async-start(), calls=%async_computation.13 | async-start | bytes 6291456 | tf_op jit(solution)/shard_map/psum | solution.py:177
  367.5 69.1 %all-reduce.13.cloned.1.call-start = ((), (), s32[]{:S(2)}) async-start(), calls=%async_computation.14 | async-start | bytes 6291456 | tf_op jit(solution)/shard_map/psum | solution.py:204
  444.5 36.4 %copy-start.13 = (bf16[4,256,384]{2,1,0:T(8,128)(2,1)}, bf16[4,256,384]{2,1,0:T(8,128)(2,1)S(1)}, u32[]{:S(2)}) copy-start(bf16[4,256,384]{2,1,0:T(8,128)(2,1)S(1)} %get-tuple-element.526) | copy-start | bytes 2359300 | tf_op jit(solution)/shard_map/while
  444.5 34.8 %all-gather.24.cloned.1.call-start = ((), (), s32[]{:S(2)}) async-start(), calls=%async_computation.26 | async-start | bytes 1966080 | tf_op jit(solution)/shard_map/while/body/eval_jaxpr/all_gather | solution.py:59
  446.6 73.6 %reduce-scatter.38.cloned.1.call-start = ((), (), s32[]{:S(2)}) async-start(), calls=%async_computation.27 | async-start | bytes 1966080 | tf_op jit(solution)/shard_map/while/body/eval_jaxpr/reduce_scatter | solution.py:103
  522.1 33.6 %all-gather.24.cloned.1.call-start = ((), (), s32[]{:S(2)}) async-start(), calls=%async_computation.26 | async-start | bytes 1966080 | tf_op jit(solution)/shard_map/while/body/eval_jaxpr/all_gather | solution.py:59
  524.2 72.4 %reduce-scatter.38.cloned.1.call-start = ((), (), s32[]{:S(2)}) async-start(), calls=%async_computation.27 | async-start | bytes 1966080 | tf_op jit(solution)/shard_map/while/body/eval_jaxpr/reduce_scatter | solution.py:103
  598.6 33.3 %all-gather.24.cloned.1.call-start = ((), (), s32[]{:S(2)}) async-start(), calls=%async_computation.26 | async-start | bytes 1966080 | tf_op jit(solution)/shard_map/while/body/eval_jaxpr/all_gather | solution.py:59
  600.6 72.1 %reduce-scatter.38.cloned.1.call-start = ((), (), s32[]{:S(2)}) async-start(), calls=%async_computation.27 | async-start | bytes 1966080 | tf_op jit(solution)/shard_map/while/body/eval_jaxpr/reduce_scatter | solution.py:103
  674.7 33.3 %all-gather.24.cloned.1.call-start = ((), (), s32[]{:S(2)}) async-start(), calls=%async_computation.26 | async-start | bytes 1966080 | tf_op jit(solution)/shard_map/while/body/eval_jaxpr/all_gather | solution.py:59
  676.8 72.1 %reduce-scatter.38.cloned.1.call-start = ((), (), s32[]{:S(2)}) async-start(), calls=%async_computation.27 | async-start | bytes 1966080 | tf_op jit(solution)/shard_map/while/body/eval_jaxpr/reduce_scatter | solution.py:103
  750.9 51.3 %reduce-scatter.36.cloned.1.call-start = ((), (), s32[]{:S(2)}) async-start(), calls=%async_computation.23 | async-start | bytes 2949120
  751.6 90.7 %reduce-scatter.26.cloned.1.call-start = ((), (), s32[]{:S(2)}) async-start(), calls=%async_computation.18 | async-start | bytes 2211840
  762.7 103.6 %reduce-scatter.22.cloned.1.call-start = ((), (), s32[]{:S(2)}) async-start(), calls=%async_computation.16 | async-start | bytes 737280 | tf_op jit(solution)/shard_map/reduce_scatter | solution.py:265
  766.2 148.9 %reduce-scatter.24.cloned.1.call-start = ((), (), s32[]{:S(2)}) async-start(), calls=%async_computation.17 | async-start | bytes 2949120 | tf_op jit(solution)/shard_map/reduce_scatter | solution.py:283
  772.5 163.2 %reduce-scatter.28.cloned.1.call-start = ((), (), s32[]{:S(2)}) async-start(), calls=%async_computation.19 | async-start | bytes 20480
  776.9 178.6 %reduce-scatter.32.cloned.1.call-start = ((), (), s32[]{:S(2)}) async-start(), calls=%async_computation.21 | async-start | bytes 245760
  777.8 198.1 %reduce-scatter.30.cloned.1.call-start = ((), (), s32[]{:S(2)}) async-start(), calls=%async_computation.20 | async-start | bytes 245760
  778.8 216.9 %reduce-scatter.34.cloned.1.call-start = ((), (), s32[]{:S(2)}) async-start(), calls=%async_computation.22 | async-start | bytes 245760
  779.7 237.4 %all-reduce.15.cloned.1.call-start = ((), (), s32[]{:S(2)}) async-start(), calls=%async_computation.15 | async-start | bytes 3145728 | tf_op jit(solution)/shard_map/psum | solution.py:245
  785.1 129.9 %copy-start.28 = (u32[32]{0:T(128)S(1)}, u32[32]{0:T(128)}, u32[]{:S(2)}) copy-start(u32[32]{0:T(128)} %constant.143) | copy-start | bytes 388
  785.2 232.0 %copy-start.4 = (f32[1024,768]{1,0:T(8,128)S(1)}, f32[1024,768]{1,0:T(8,128)}, u32[]{:S(2)}) copy-start(f32[1024,768]{1,0:T(8,128)} %copy-done.3) | copy-start | bytes 9437188
  785.2 305.1 %all-reduce.17.cloned.1.call-start = ((), (), s32[]{:S(2)}) async-start(), calls=%async_computation.24 | async-start | bytes 3833856 | tf_op jit(solution)/shard_map/psum | solution.py:288
  (42 other events, 396.7 us)
Sparse Core Ops, SparseCore 0:
  9.6 52.4 all-gather.15
  71.1 29.6 all-gather.21
  111.0 30.8 all-gather.21
  151.8 30.8 all-gather.21
  192.6 30.8 all-gather.21
  233.3 23.1 all-reduce.8
  258.2 51.4 all-gather.17
  311.4 49.2 all-gather.19
  367.7 22.0 all-reduce.10
  412.2 24.3 all-reduce.12
  447.3 31.9 all-gather.23
  489.2 30.9 reduce-scatter.37
  524.9 30.7 all-gather.23
  565.6 30.9 reduce-scatter.37
  601.1 30.7 all-gather.23
  641.7 30.9 reduce-scatter.37
  677.2 30.7 all-gather.23
  717.9 30.9 reduce-scatter.37
  754.1 47.9 reduce-scatter.35
  804.4 37.8 reduce-scatter.25
  845.2 21.0 reduce-scatter.21
  868.6 46.3 reduce-scatter.23
  917.3 18.3 reduce-scatter.27
  937.9 17.4 reduce-scatter.31
  958.3 17.6 reduce-scatter.29
  978.1 17.4 reduce-scatter.33
  998.4 18.6 all-reduce.14
  1021.6 68.6 all-reduce.16
where the time goes:
time: 1110 us; the launch traced here: 1100 us
  waiting for transfers between devices  729 us (66%)
  matrix products  119 us (11%)
  blocking collectives  99.4 us (9%)
  local copies, waits for them, and re-layouts  86.6 us (8%)
  other arithmetic  50.7 us (5%)
  between operations  15.8 us (1%)
    unnamed x22, waiting for transfers between devices  125 us
    all_gather x4, waiting for transfers between devices, attend_slot(): gathered = lax.all_gather(key_value, 'ctx', axis=1, tiled=True)  123 us
    all_gather x4, waiting for transfers between devices, slot_grads(): gathered = lax.all_gather(key_value, 'ctx', axis=1, tiled=True)  117 us
    reduce_scatter x4, waiting for transfers between devices, slot_grads(): lax.psum_scatter(key_terms.astype(jnp.bfloat16), 'ctx', scatter_dimension...  108 us
    psum x1, waiting for transfers between devices, per_device(): lax.psum(shares[0].astype(jnp.bfloat16), 'ctx').astype(jnp.float32)  70.2 us
    reduce_scatter x1, waiting for transfers between devices, per_device(): lax.psum_scatter(grad_down.astype(jnp.bfloat16), 'fsdp', scatter_dimensio...  48.7 us
    unnamed x88, local copies, waits for them, and re-layouts  34.5 us
    all_gather x1, waiting for transfers between devices, per_device(): lax.all_gather(w_ffo, 'fsdp', axis=0, tiled=True)  31.3 us
  transfers between devices with their start and end apart: 28, of which 27 were waited for; matrix products, arithmetic and copies ran while one was open for 10% of the time, Pallas kernels for 0%

commit v1 on v0

--- a/solution.py
+++ b/solution.py
@@ -1,7 +1,818 @@
+import functools
+
 import jax
 import jax.numpy as jnp
 from jax import lax
+from jax.experimental import pallas as pl
+from jax.experimental.pallas import tpu as pltpu
 from jax.sharding import PartitionSpec as P
+
+f32 = jnp.float32
+bf16 = jnp.bfloat16
+MESH = pl.DeviceIdType.MESH
+ANY = pl.BlockSpec(memory_space=pl.ANY)
+VM = pl.BlockSpec(memory_space=pltpu.VMEM)
+SM = pl.BlockSpec(memory_space=pltpu.SMEM)
+DMA = pltpu.SemaphoreType.DMA
+NN = (((1,), (0,)), ((), ()))
+NT = (((1,), (1,)), ((), ()))
+TN = (((0,), (0,)), ((), ()))
+VMEM_BYTES = 60 << 20
+
+
+def dot(left, right, dims=NN):
+    return lax.dot_general(left, right, dims, preferred_element_type=f32)
+
+
+def struct(shape, dtype):
+    return jax.ShapeDtypeStruct(shape, dtype)
+
+
+def place():
+    z, c, t = lax.axis_index("fsdp"), lax.axis_index("ctx"), lax.axis_index("tp")
+    along_x = c + 1 - 2 * (c % 2)
+    along_y = c + 2 - 4 * (c // 2)
+    n1 = along_x + t * (along_y - along_x)
+    n2 = along_y + t * (along_x - along_y)
+    return z, c, t, n1, n2, 3 - c
+
+
+def remote(src, dst, send_sem, recv_sem, device):
+    return pltpu.make_async_remote_copy(
+        src_ref=src,
+        dst_ref=dst,
+        send_sem=send_sem,
+        recv_sem=recv_sem,
+        device_id=device,
+        device_id_type=MESH,
+    )
+
+
+def meet(devices):
+    barrier = pltpu.get_barrier_semaphore()
+    for device in devices:
+        pl.semaphore_signal(barrier, inc=1, device_id=device, device_id_type=MESH)
+    pl.semaphore_wait(barrier, len(devices))
+
+
+def tile(i, size):
+    return pl.ds(pl.multiple_of(i * size, size), size)
+
+
+def gather_kernel(
+    x_in, og_in, qkv_in, out_in, up_in, down_in, small_in,
+    xs, ogs, qkv, wout, wup, wdown, small,
+    loc, xsend, xrecv, osend, orecv, fsend, frecv, zsend, zrecv, asend, arecv, bsend, brecv, csend, crecv,
+):
+    z, c, t, n1, n2, dg = place()
+    half = 128
+    planes = (n1, n2, dg)
+    meet(
+        [(z, p, t) for p in planes]
+        + [((z + d) % 4, c, t) for d in (1, 2, 3)]
+        + [(z, c, 1 - t)]
+    )
+
+    def region(w, zz, q):
+        if w == 0:
+            return qkv.at[:, pl.ds(pl.multiple_of(zz * 192 + q * 48, 16), 48), :]
+        if w == 1:
+            return wout.at[zz, tile(q, 96), :]
+        if w == 2:
+            return wup.at[zz, tile(q, 192), :]
+        if w == 3:
+            return wdown.at[zz, tile(q, 96), :]
+        return small.at[zz]
+
+    def mine(w):
+        if w == 0:
+            return qkv_in.at[:, tile(c, 48), :]
+        if w == 1:
+            return out_in.at[tile(c, 96), :]
+        if w == 2:
+            return up_in.at[tile(c, 192), :]
+        if w == 3:
+            return down_in.at[tile(c, 96), :]
+        return small_in
+
+    pending = []
+    xcopies = []
+    for i, p in enumerate(planes):
+        cp = remote(x_in.at[p, tile(t, half), :], xs.at[t, c], xsend.at[i], xrecv.at[i], (z, p, t))
+        cp.start()
+        xcopies.append(cp)
+    zcopies = {}
+
+    def send_z(w):
+        for d in (1, 2, 3):
+            cp = remote(mine(w), region(w, z, c), zsend.at[w, d - 1], zrecv.at[w, d - 1], ((z + d) % 4, c, t))
+            cp.start()
+            zcopies[w, d] = cp
+
+    send_z(0)
+    send_z(4)
+    send_z(1)
+    send_z(2)
+    send_z(3)
+    local = [
+        pltpu.make_async_copy(x_in.at[c, pl.ds(0, half), :], xs.at[0, c], loc.at[0]),
+        pltpu.make_async_copy(x_in.at[c, pl.ds(half, half), :], xs.at[1, c], loc.at[1]),
+        pltpu.make_async_copy(og_in.at[c, tile(t, half), :], ogs.at[c], loc.at[2]),
+        pltpu.make_async_copy(qkv_in, qkv.at[:, tile(z, 192), :], loc.at[3]),
+        pltpu.make_async_copy(out_in, wout.at[z], loc.at[4]),
+        pltpu.make_async_copy(up_in, wup.at[z], loc.at[5]),
+        pltpu.make_async_copy(down_in, wdown.at[z], loc.at[6]),
+        pltpu.make_async_copy(small_in, small.at[z], loc.at[7]),
+    ]
+    for cp in local:
+        cp.start()
+
+    def spread(w):
+        for d in (1, 2, 3):
+            zcopies[w, d].wait_recv()
+            zz = (z + 4 - d) % 4
+            a = remote(region(w, zz, c), region(w, zz, c), asend.at[w, d - 1], arecv.at[w, d - 1], (z, n1, t))
+            b = remote(region(w, zz, c), region(w, zz, c), bsend.at[w, d - 1], brecv.at[w, d - 1], (z, n2, t))
+            a.start()
+            b.start()
+            pending.append((w, d, a, b))
+
+    ccopies = []
+
+    def finish(w):
+        for w_, d, a, b in pending:
+            if w_ == w:
+                a.wait_recv()
+                zz = (z + 4 - d) % 4
+                cc = remote(region(w, zz, n1), region(w, zz, n1), csend.at[w, d - 1], crecv.at[w, d - 1], (z, n2, t))
+                cc.start()
+                ccopies.append(cc)
+
+    spread(0)
+    forwards = []
+    for i, p in enumerate(planes):
+        xcopies[i].wait_recv()
+        cp = remote(xs.at[t, p], xs.at[t, p], fsend.at[i], frecv.at[i], (z, c, 1 - t))
+        cp.start()
+        forwards.append(cp)
+    spread(1)
+    finish(0)
+    spread(2)
+    finish(1)
+    spread(3)
+    finish(2)
+    ocopies = []
+    for i, p in enumerate(planes):
+        cp = remote(og_in.at[p, tile(t, half), :], ogs.at[c], osend.at[i], orecv.at[i], (z, p, t))
+        cp.start()
+        ocopies.append(cp)
+    finish(3)
+    for cp in local:
+        cp.wait()
+    for cp in xcopies:
+        cp.wait_send()
+    for cp in ocopies + forwards:
+        cp.wait()
+    for (w, d), cp in zcopies.items():
+        cp.wait_send()
+        if w == 4:
+            cp.wait_recv()
+    for w, d, a, b in pending:
+        a.wait_send()
+        b.wait()
+    for cp in ccopies:
+        cp.wait()
+
+
+def gather(x, og, w_qkv, w_out, w_in, w_ffo, small):
+    return pl.pallas_call(
+        gather_kernel,
+        out_shape=(
+            struct((2, 4, 128, 768), bf16),
+            struct((4, 128, 768), bf16),
+            struct((3, 768, 384), bf16),
+            struct((4, 384, 192), bf16),
+            struct((4, 768, 384), bf16),
+            struct((4, 384, 768), bf16),
+            struct((4, 16, 384), f32),
+        ),
+        in_specs=[ANY] * 7,
+        out_specs=[ANY] * 7,
+        scratch_shapes=[
+            DMA((8,)), DMA((3,)), DMA((3,)), DMA((3,)), DMA((3,)), DMA((3,)), DMA((3,)),
+            DMA((5, 3)), DMA((5, 3)), DMA((4, 3)), DMA((4, 3)), DMA((4, 3)), DMA((4, 3)), DMA((4, 3)), DMA((4, 3)),
+        ],
+        compiler_params=pltpu.CompilerParams(collective_id=0, has_side_effects=True),
+        name="gather",
+    )(x, og, w_qkv, w_out, w_in, w_ffo, small)
+
+
+def split3(v):
+    hi = v.astype(bf16).astype(f32)
+    rest = v - hi
+    mid = rest.astype(bf16).astype(f32)
+    return hi, mid, rest - mid
+
+
+def key_bias(length, rows):
+    r = lax.broadcasted_iota(jnp.int32, (rows, 128), 0)
+    position = (r % 512) // 128 * 256 + r // 512 * 128 + r % 128
+    return jnp.where(position < length, 0.0, -1e30)
+
+
+def attend_forward(q_ref, k_ref, v_ref, kb, out_ref, lse_ref, qe, ke, ve, block):
+    rows_all = q_ref.shape[0]
+    lane = lax.broadcasted_iota(jnp.int32, (rows_all, 128), 1)
+    lse_ref[...] = jnp.zeros_like(lse_ref)
+
+    def pair(hp, _):
+        cols = tile(hp, 128)
+        q, k, v = q_ref[:, cols].astype(f32), k_ref[:, cols].astype(f32), v_ref[:, cols].astype(f32)
+        for j in range(2):
+            own = (lane < 64) if j == 0 else (lane >= 64)
+            e = 64 if j == 0 else 0
+            one = jnp.where(lane == e, 1.0, 0.0)
+            qe[j] = jnp.where(own, q, one).astype(bf16)
+            ke[j] = jnp.where(own, k, jnp.where(lane == e, kb, 0.0)).astype(bf16)
+            ve[j] = jnp.where(own, v, one).astype(bf16)
+
+        def query_block(b, _):
+            rows = tile(b, block)
+            ln = lax.broadcasted_iota(jnp.int32, (block, 128), 1)
+            outs, totals = [], []
+            for j in range(2):
+                e = 64 if j == 0 else 0
+                s = dot(qe[j, rows, :], ke[j], NT)
+                m = jnp.max(s, axis=1, keepdims=True)
+                p = jnp.exp(s - m).astype(bf16)
+                o = dot(p, ve[j])
+                total = o[:, e : e + 1]
+                outs.append(o * (1.0 / total))
+                totals.append(m + jnp.log(total))
+            out_ref[rows, cols] = jnp.where(ln < 64, outs[0], outs[1]).astype(bf16)
+            cur = lse_ref[rows, :]
+            cur = jnp.where(ln == 2 * hp, totals[0], cur)
+            lse_ref[rows, :] = jnp.where(ln == 2 * hp + 1, totals[1], cur)
+            return 0
+
+        lax.fori_loop(0, rows_all // block, query_block, 0)
+        return 0
+
+    lax.fori_loop(0, q_ref.shape[1] // 128, pair, 0)
+
+
+def attend_backward(
+    q_ref, k_ref, v_ref, kb, mixed_ref, do_ref, lse_ref, dq_ref, dk_ref, dv_ref, qe, ke, ve, de, qz, dz, kt, dqt, block
+):
+    rows_all = q_ref.shape[0]
+    lane = lax.broadcasted_iota(jnp.int32, (rows_all, 128), 1)
+
+    def pair(hp, _):
+        cols = tile(hp, 128)
+        q, k, v = q_ref[:, cols].astype(f32), k_ref[:, cols].astype(f32), v_ref[:, cols].astype(f32)
+        do = do_ref[:, cols].astype(f32)
+        pr = do * mixed_ref[:, cols].astype(f32)
+        lse_all = lse_ref[...]
+        for j in range(2):
+            own = (lane < 64) if j == 0 else (lane >= 64)
+            e = 64 if j == 0 else 0
+            delta = jnp.sum(jnp.where(own, pr, 0.0), axis=1, keepdims=True)
+            lse = jnp.sum(jnp.where(lane == 2 * hp + j, lse_all, 0.0), axis=1, keepdims=True)
+            lh, lm, ll = split3(-lse)
+            dh, dm, dl = split3(-delta)
+            qz[j] = jnp.where(own, q, 0.0).astype(bf16)
+            dz[j] = jnp.where(own, do, 0.0).astype(bf16)
+            side = jnp.where(lane == e, 1.0, 0.0)
+            side = jnp.where(lane == e + 1, lh, side)
+            side = jnp.where(lane == e + 2, lm, side)
+            side = jnp.where(lane == e + 3, ll, side)
+            qe[j] = jnp.where(own, q, side).astype(bf16)
+            ones3 = jnp.where((lane > e) & (lane < e + 4), 1.0, 0.0)
+            ke[j] = jnp.where(own, k, jnp.where(lane == e, kb, ones3)).astype(bf16)
+            side = jnp.where(lane == e + 1, dh, 0.0)
+            side = jnp.where(lane == e + 2, dm, side)
+            side = jnp.where(lane == e + 3, dl, side)
+            de[j] = jnp.where(own, do, side).astype(bf16)
+            ve[j] = jnp.where(own, v, ones3).astype(bf16)
+        kt[...] = k.T.astype(bf16)
+        dqt[...] = jnp.zeros_like(dqt)
+
+        def key_block(b, _):
+            rows = tile(b, block)
+            dv, dk = None, None
+            for j in range(2):
+                p = jnp.exp(dot(ke[j, rows, :], qe[j], NT))
+                g = dot(ve[j, rows, :], de[j], NT)
+                ds = (p * g).astype(bf16)
+                a = dot(p.astype(bf16), dz[j])
+                b_ = dot(ds, qz[j])
+                dv = a if dv is None else dv + a
+                dk = b_ if dk is None else dk + b_
+                dqt[64 * j : 64 * j + 64, :] += dot(kt[64 * j : 64 * j + 64, rows], ds)
+            dk_ref[rows, cols] = dk.astype(bf16)
+            dv_ref[rows, cols] = dv.astype(bf16)
+            return 0
+
+        lax.fori_loop(0, rows_all // block, key_block, 0)
+        dq_ref[:, cols] = (dqt[...] * 0.125).T.astype(bf16)
+        return 0
+
+    lax.fori_loop(0, q_ref.shape[1] // 128, pair, 0)
+
+
+def forward_kernel(len_ref, xs, wqkv, bias, q_ref, k_ref, v_ref, mixed, lse, qe, ke, ve):
+    c = lax.axis_index("ctx")
+
+    def project(i, _):
+        rows = tile(i, 256)
+        xr = xs[rows, :]
+        q_ref[rows, :] = ((dot(xr, wqkv[0]) + bias[0:1, :]).astype(bf16).astype(f32) * 0.125).astype(bf16)
+        k_ref[rows, :] = dot(xr, wqkv[1]).astype(bf16)
+        v_ref[rows, :] = (dot(xr, wqkv[2]) + bias[1:2, :]).astype(bf16)
+        return 0
+
+    lax.fori_loop(0, 4, project, 0)
+    attend_forward(q_ref, k_ref, v_ref, key_bias(len_ref[c], 1024), mixed, lse, qe, ke, ve, 512)
+
+
+def forward(lengths, xs, wqkv, bias):
+    return pl.pallas_call(
+        forward_kernel,
+        out_shape=(struct((1024, 384), bf16),) * 4 + (struct((1024, 128), f32),),
+        in_specs=[SM, VM, VM, VM],
+        scratch_shapes=[pltpu.VMEM((2, 1024, 128), bf16)] * 3,
+        compiler_params=pltpu.CompilerParams(vmem_limit_bytes=VMEM_BYTES),
+        name="attention_forward",
+    )(lengths, xs, wqkv, bias)
+
+
+def backward_kernel(
+    len_ref, xs, wqkv, q_ref, k_ref, v_ref, mixed, gmixed, lse, gres,
+    dxown, dxother, gqkv, gbias, dq, dk, dv, qe, ke, ve, de, qz, dz, kt, dqt,
+):
+    c, t = lax.axis_index("ctx"), lax.axis_index("tp")
+    attend_backward(
+        q_ref, k_ref, v_ref, key_bias(len_ref[c], 1024), mixed, gmixed, lse, dq, dk, dv, qe, ke, ve, de, qz, dz, kt, dqt, 512
+    )
+
+    def rows_back(i, _):
+        h = (i // 2 + 1 - t) % 2
+        rows = pl.ds(pl.multiple_of(h * 512 + i % 2 * 256, 256), 256)
+        part = dot(dq[rows, :], wqkv[0], NT) + dot(dk[rows, :], wqkv[1], NT) + dot(dv[rows, :], wqkv[2], NT)
+
+        @pl.when(i < 2)
+        def _():
+            dxother[tile(i % 2, 256), :] = part
+
+        @pl.when(i >= 2)
+        def _():
+            dxown[tile(i % 2, 256), :] = part + gres[tile(i % 2, 256), :]
+
+        return 0
+
+    lax.fori_loop(0, 4, rows_back, 0)
+
+    def weights(i, _):
+        xr = xs[:, tile(i, 128)]
+        for p, g in enumerate((dq, dk, dv)):
+            gqkv[p, tile(i, 128), :] = dot(xr, g[...], TN).astype(bf16)
+        return 0
+
+    lax.fori_loop(0, 6, weights, 0)
+    gbias[...] = jnp.zeros_like(gbias)
+    gbias[0:1, :] = jnp.sum(dq[...].astype(f32), axis=0, keepdims=True)
+    gbias[1:2, :] = jnp.sum(dv[...].astype(f32), axis=0, keepdims=True)
+
+
+def backward(lengths, xs, wqkv, q, k, v, mixed, gmixed, lse, gres):
+    half = pltpu.VMEM((2, 1024, 128), bf16)
+    return pl.pallas_call(
+        backward_kernel,
+        out_shape=(struct((512, 768), f32), struct((512, 768), f32), struct((3, 768, 384), bf16), struct((8, 384), f32)),
+        in_specs=[SM] + [VM] * 9,
+        scratch_shapes=[pltpu.VMEM((1024, 384), bf16)] * 3
+        + [half] * 6
+        + [pltpu.VMEM((128, 1024), bf16), pltpu.VMEM((128, 1024), f32)],
+        compiler_params=pltpu.CompilerParams(vmem_limit_bytes=VMEM_BYTES),
+        name="attention_backward",
+    )(lengths, xs, wqkv, q, k, v, mixed, gmixed, lse, gres)
+
+
+def gelu_pair(h):
+    cdf = 0.5 * (1.0 + lax.erf(h * 0.7071067811865476))
+    density = jnp.exp(h * h * -0.5) * 0.3989422804014327
+    return h * cdf, cdf + h * density
+
+
+def unit_rows(r):
+    centred = r - jnp.mean(r, axis=-1, keepdims=True)
+    spread = jnp.mean(centred * centred, axis=-1, keepdims=True)
+    inverse = lax.rsqrt(spread + 1e-5)
+    return centred * inverse, inverse
+
+
+def norm_back(g, n, inverse):
+    return inverse * (g - jnp.mean(g, axis=-1, keepdims=True) - n * jnp.mean(g * n, axis=-1, keepdims=True))
+
+
+def column_sum(v):
+    return jnp.sum(v, axis=0, keepdims=True)
+
+
+def middle_kernel(
+    len_ref, mixed, xs, ogs, wout4, wup, wdown, rowp, upb,
+    hout, gres, gmixed, gup, gdown, gout, grow, gupb,
+    wout, part, parta, partb, partc, recva, recvb, recvc, n1r, n2r, inv1, inv2, low1, low2, low3, act, slope, ghid, g2r,
+    send, recv,
+):
+    c, t = lax.axis_index("ctx"), lax.axis_index("tp")
+    z = lax.axis_index("fsdp")
+    sibling = (z, c, 1 - t)
+    meet([sibling])
+    u = 1 - t
+    copies = []
+
+    def exchange(stage, i, src, dst):
+        cp = remote(src, dst, send.at[stage, i], recv.at[stage, i], sibling)
+        cp.start()
+        copies.append(cp)
+        return cp
+
+    for j in range(4):
+        spot = lax.broadcasted_iota(jnp.int32, (192, 768), 1) == lax.broadcasted_iota(jnp.int32, (192, 768), 0) + 192 * j
+        piece = dot(wout4[j], jnp.where(spot, 1.0, 0.0).astype(bf16))
+        if j == 0:
+            part[...] = piece
+        else:
+            part[...] += piece
+    wout[...] = part[...].astype(bf16)
+    bias0, bias1 = rowp[0:1, :], rowp[1:2, :]
+    gain0, gain1 = rowp[2:3, :], rowp[3:4, :]
+    shift0, shift1 = rowp[4:5, :], rowp[5:6, :]
+
+    def rows_of(h, i):
+        return pl.ds(pl.multiple_of(h * 512 + i * 256, 256), 256)
+
+    a = []
+    for i in range(2):
+        parta[i] = dot(mixed[rows_of(u, i), :], wout[...])
+        a.append(exchange(0, i, parta.at[i], recva.at[i]))
+    for i in range(2):
+        parta[2 + i] = dot(mixed[rows_of(t, i), :], wout[...])
+    b = []
+    for i in range(2):
+        a[i].wait_recv()
+        r = xs[rows_of(t, i), :].astype(f32) + (parta[2 + i] + recva[i] + bias0)
+        n, inverse = unit_rows(r)
+        n1r[i] = n
+        inv1[i] = jnp.broadcast_to(inverse, (256, 128))
+        low1[t, i] = (n * gain0 + shift0).astype(bf16)
+        b.append(exchange(1, i, low1.at[t, i], low1.at[t, i]))
+
+    def up(h, i):
+        def chunk(zz, _):
+            hidden = dot(low1[h, i], wup[zz]) + upb[pl.ds(zz, 1), :]
+            value, grad = gelu_pair(hidden)
+            act[zz, rows_of(h, i), :] = value.astype(bf16)
+            slope[zz, rows_of(h, i), :] = grad.astype(bf16)
+            return 0
+
+        lax.fori_loop(0, 4, chunk, 0)
+
+    up(t, 0)
+    up(t, 1)
+    b[0].wait_recv()
+    up(u, 0)
+    b[1].wait_recv()
+    up(u, 1)
+
+    def down(h, i, target):
+        rows = rows_of(h, i)
+        total = dot(act[0, rows, :], wdown[0])
+        for zz in range(1, 4):
+            total += dot(act[zz, rows, :], wdown[zz])
+        target[...] = total
+
+    a = []
+    for i in range(2):
+        down(u, i, partb.at[i])
+        a.append(exchange(2, i, partb.at[i], recvb.at[i]))
+    for i in range(2):
+        down(t, i, partb.at[2 + i])
+    b = []
+    gg1 = gs1 = gb1 = 0.0
+    for i in range(2):
+        a[i].wait_recv()
+        n, inverse = unit_rows((n1r[i] * gain0 + shift0) + (partb[2 + i] + recvb[i] + bias1))
+        hout[pl.ds(256 * i, 256), :] = (n * gain1 + shift1).astype(bf16)
+        r = lax.broadcasted_iota(jnp.int32, (256, 768), 0) + 256 * i
+        live = (r // 128 * 256 + t * 128 + r % 128) < len_ref[c]
+        g = jnp.where(live, ogs[pl.ds(256 * i, 256), :].astype(f32), 0.0)
+        gg1 = gg1 + column_sum(g * n)
+        gs1 = gs1 + column_sum(g)
+        g2 = norm_back(g * gain1, n, inverse)
+        g2r[i] = g2
+        low2[t, i] = g2.astype(bf16)
+        b.append(exchange(3, i, low2.at[t, i], low2.at[t, i]))
+        gb1 = gb1 + column_sum(low2[t, i].astype(f32))
+
+    gupb[...] = jnp.zeros_like(gupb)
+
+    def back(h, i):
+        def chunk(zz, _):
+            rows = rows_of(h, i)
+            g = (dot(low2[h, i], wdown[zz], NT) * slope[zz, rows, :].astype(f32)).astype(bf16)
+            ghid[zz, rows, :] = g
+            gupb[pl.ds(zz, 1), :] += column_sum(g.astype(f32))
+            return 0
+
+        lax.fori_loop(0, 4, chunk, 0)
+
+    back(t, 0)
+    back(t, 1)
+    b[0].wait_recv()
+    back(u, 0)
+    b[1].wait_recv()
+    back(u, 1)
+
+    def first_grad(h, i, target):
+        rows = rows_of(h, i)
+        total = dot(ghid[0, rows, :], wup[0], NT)
+        for zz in range(1, 4):
+            total += dot(ghid[zz, rows, :], wup[zz], NT)
+        target[...] = total
+
+    a = []
+    for i in range(2):
+        first_grad(u, i, partc.at[i])
+        a.append(exchange(4, i, partc.at[i], recvc.at[i]))
+    for i in range(2):
+        first_grad(t, i, partc.at[2 + i])
+    b = []
+    gg0 = gs0 = gb0 = 0.0
+    for i in range(2):
+        a[i].wait_recv()
+        g1 = g2r[i] + (partc[2 + i] + recvc[i])
+        n = n1r[i]
+        gg0 = gg0 + column_sum(g1 * n)
+        gs0 = gs0 + column_sum(g1)
+        g = norm_back(g1 * gain0, n, inv1[i][:, 0:1])
+        gres[pl.ds(256 * i, 256), :] = g
+        low3[t, i] = g.astype(bf16)
+        b.append(exchange(5, i, low3.at[t, i], low3.at[t, i]))
+        gb0 = gb0 + column_sum(low3[t, i].astype(f32))
+    for k, v in enumerate((gb0, gb1, gg0, gg1, gs0, gs1)):
+        grow[k : k + 1, :] = v
+    grow[6:8, :] = jnp.zeros((2, 768), f32)
+
+    def weights(zz, _):
+        for k in range(3):
+            down_rows = pl.ds(128 * k, 128)
+            g = dot(act[zz, :, down_rows], low2[...].reshape(1024, 768), TN)
+            gdown[zz, down_rows, :] = g.astype(bf16)
+        for k in range(6):
+            up_rows = pl.ds(128 * k, 128)
+            g = dot(low1[:, :, :, up_rows].reshape(1024, 128), ghid[zz], TN)
+            gup[zz, up_rows, :] = g.astype(bf16)
+        return 0
+
+    lax.fori_loop(0, 4, weights, 0)
+    b[0].wait_recv()
+    b[1].wait_recv()
+    for h in range(2):
+        for i in range(2):
+            gmixed[rows_of(h, i), :] = dot(low3[h, i], wout[...], NT).astype(bf16)
+    for k in range(3):
+        mixed_rows = pl.ds(128 * k, 128)
+        part[mixed_rows, :] = dot(mixed[:, mixed_rows], low3[...].reshape(1024, 768), TN)
+    for j in range(4):
+        gout[j] = part[:, 192 * j : 192 * j + 192].astype(bf16)
+    for cp in copies:
+        cp.wait_send()
+
+
+def middle(lengths, mixed, xs, ogs, wout4, wup, wdown, rowp, upb):
+    rows2 = pltpu.VMEM((2, 256, 768), f32)
+    low = pltpu.VMEM((2, 2, 256, 768), bf16)
+    wide = pltpu.VMEM((4, 1024, 384), bf16)
+    return pl.pallas_call(
+        middle_kernel,
+        out_shape=(
+            struct((512, 768), bf16),
+            struct((512, 768), f32),
+            struct((1024, 384), bf16),
+            struct((4, 768, 384), bf16),
+            struct((4, 384, 768), bf16),
+            struct((4, 384, 192), bf16),
+            struct((8, 768), f32),
+            struct((4, 384), f32),
+        ),
+        in_specs=[SM] + [VM] * 8,
+        scratch_shapes=[
+            pltpu.VMEM((384, 768), bf16),
+            pltpu.VMEM((384, 768), f32),
+            pltpu.VMEM((4, 256, 768), f32), pltpu.VMEM((4, 256, 768), f32), pltpu.VMEM((4, 256, 768), f32),
+            rows2, rows2, rows2, rows2, rows2,
+            pltpu.VMEM((2, 256, 128), f32), pltpu.VMEM((2, 256, 128), f32),
+            low, low, low, wide, wide, wide, rows2,
+            DMA((6, 2)), DMA((6, 2)),
+        ],
+        compiler_params=pltpu.CompilerParams(collective_id=1, has_side_effects=True, vmem_limit_bytes=VMEM_BYTES),
+        name="rows",
+    )(lengths, mixed, xs, ogs, wout4, wup, wdown, rowp, upb)
+
+
+def reduce_kernel(
+    gqkv, gout, gup, gdown, gsmall, hout, dxown, dxother,
+    oqkv, oout, oup, odown, osmall, oh, odx,
+    r0, r1, r2, r3, s0, s1, s2, s3, z0, z1, z2, z3, sms, sm, smt, smr, smc, dxr, dxl,
+    lsem, s1s, s1r, s2s, s2r, s3s, s3r, s4s, s4r, ms, mr, hs, hr, fs, fr,
+):
+    z, c, t, n1, n2, dg = place()
+    sibling = (z, c, 1 - t)
+    planes = (n1, n2, dg)
+    meet([(z, p, t) for p in planes] + [((z + d) % 4, c, t) for d in (1, 2, 3)] + [sibling])
+    grads = (gqkv, gout, gup, gdown)
+    outs = (oqkv, oout, oup, odown)
+    first = (r0, r1, r2, r3)
+    second = (s0, s1, s2, s3)
+    third = (z0, z1, z2, z3)
+    quarter_rows = (48, 96, 192, 96)
+    order = (3, 2, 1, 0)
+    sends = []
+
+    def go(src, dst, ss, rs, device):
+        cp = remote(src, dst, ss, rs, device)
+        cp.start()
+        sends.append(cp)
+        return cp
+
+    def grad(w, q):
+        rows = tile(q, quarter_rows[w])
+        return grads[w].at[:, :, rows, :] if w == 0 else grads[w].at[:, rows, :]
+
+    def shard(w, ref, zz):
+        return ref.at[:, zz] if w == 0 else ref.at[zz]
+
+    def out(w, q):
+        rows = tile(q, quarter_rows[w])
+        return outs[w].at[:, rows, :] if w == 0 else outs[w].at[rows, :]
+
+    xch = go(dxother, dxr, ms.at[0], mr.at[0], sibling)
+    xsm = go(gsmall, sms, ms.at[1], mr.at[1], sibling)
+    stage1 = {}
+    for w in order:
+        stage1[w] = [
+            go(grad(w, n1), first[w].at[0], s1s.at[w, 0], s1r.at[w, 0], (z, n1, t)),
+            go(grad(w, dg), first[w].at[1], s1s.at[w, 1], s1r.at[w, 1], (z, n1, t)),
+        ]
+    hcopies = [go(hout.at[p], oh.at[c, tile(t, 128), :], hs.at[0, i], hr.at[0, i], (z, p, t)) for i, p in enumerate(planes)]
+    local = [pltpu.make_async_copy(hout.at[c], oh.at[c, tile(t, 128), :], lsem.at[0])]
+    local[0].start()
+    selfs = [go(hout.at[c], oh.at[c, tile(t, 128), :], hs.at[0, 3], hr.at[0, 3], sibling)]
+    xch.wait_recv()
+    dxl[...] = (dxown[...] + dxr[...]).astype(bf16)
+    dcopies = [go(dxl.at[p], odx.at[c, tile(t, 128), :], hs.at[1, i], hr.at[1, i], (z, p, t)) for i, p in enumerate(planes)]
+    local.append(pltpu.make_async_copy(dxl.at[c], odx.at[c, tile(t, 128), :], lsem.at[1]))
+    local[1].start()
+    selfs.append(go(dxl.at[c], odx.at[c, tile(t, 128), :], hs.at[1, 3], hr.at[1, 3], sibling))
+    xsm.wait_recv()
+    shared = lax.broadcasted_iota(jnp.int32, (4, 16, 384), 1) < 6
+    sm[...] = gsmall[...] + jnp.where(shared, sms[...], 0.0)
+    small1 = [go(sm.at[(z + d) % 4], smr.at[d], ms.at[1 + d], mr.at[1 + d], ((z + d) % 4, c, t)) for d in (1, 2, 3)]
+    stage2 = {}
+    for w in order:
+        stage1[w][1].wait_recv()
+        first[w][1] = (grad(w, n2)[...].astype(f32) + first[w][1].astype(f32)).astype(bf16)
+        stage2[w] = go(first[w].at[1], second[w].at[1], s2s.at[w], s2r.at[w], (z, n2, t))
+        stage1[w][0].wait_recv()
+        second[w][0] = (grad(w, c)[...].astype(f32) + first[w][0].astype(f32)).astype(bf16)
+    for cp in small1:
+        cp.wait_recv()
+    smt[...] = (sm[z] + smr[1]) + (smr[2] + smr[3])
+    small2 = [go(smt, smc.at[i], ms.at[5 + i], mr.at[5 + i], (z, p, t)) for i, p in enumerate(planes)]
+    stage3 = {}
+    for w in order:
+        stage2[w].wait_recv()
+        second[w][0] = (second[w][0].astype(f32) + second[w][1].astype(f32)).astype(bf16)
+        stage3[w] = [
+            go(
+                shard(w, second[w].at[0], (z + d) % 4), third[w].at[d - 1],
+                s3s.at[w, d - 1], s3r.at[w, d - 1], ((z + d) % 4, c, t),
+            )
+            for d in (1, 2, 3)
+        ]
+    fcopies = []
+    for i, p in enumerate(planes):
+        hcopies[i].wait_recv()
+        fcopies.append(go(oh.at[p, tile(t, 128), :], oh.at[p, tile(t, 128), :], fs.at[0, i], fr.at[0, i], sibling))
+        dcopies[i].wait_recv()
+        fcopies.append(go(odx.at[p, tile(t, 128), :], odx.at[p, tile(t, 128), :], fs.at[1, i], fr.at[1, i], sibling))
+    stage4 = []
+    across = {}
+    for w in order:
+        for cp in stage3[w]:
+            cp.wait_recv()
+        mine = shard(w, second[w].at[0], z)[...].astype(f32)
+        v = (mine + third[w][0].astype(f32)) + (third[w][1].astype(f32) + third[w][2].astype(f32))
+        out(w, c)[...] = v.astype(bf16)
+        across[w] = go(out(w, c), out(w, c), s4s.at[w, 0], s4r.at[w, 0], (z, n1, t))
+        stage4.append(go(out(w, c), out(w, c), s4s.at[w, 1], s4r.at[w, 1], (z, n2, t)))
+    for w in order:
+        across[w].wait_recv()
+        stage4.append(go(out(w, n1), out(w, n1), s4s.at[w, 2], s4r.at[w, 2], (z, n2, t)))
+    for cp in small2:
+        cp.wait_recv()
+    osmall[...] = (smt[...] + smc[0]) + (smc[1] + smc[2])
+    for cp in fcopies + stage4 + selfs:
+        cp.wait_recv()
+    for cp in local:
+        cp.wait()
+    for cp in sends:
+        cp.wait_send()
+
+
+def reduce(gqkv, gout, gup, gdown, gsmall, hout, dxown, dxother):
+    quarters = ((3, 4, 48, 384), (4, 96, 192), (4, 192, 384), (4, 96, 768))
+    shards = ((3, 48, 384), (96, 192), (192, 384), (96, 768))
+    return pl.pallas_call(
+        reduce_kernel,
+        out_shape=(
+            struct((3, 192, 384), bf16),
+            struct((384, 192), bf16),
+            struct((768, 384), bf16),
+            struct((384, 768), bf16),
+            struct((16, 384), f32),
+            struct((4, 256, 768), bf16),
+            struct((4, 256, 768), bf16),
+        ),
+        in_specs=[VM] * 8,
+        out_specs=(VM,) * 5 + (ANY, ANY),
+        scratch_shapes=[pltpu.VMEM((2,) + q, bf16) for q in quarters] * 2
+        + [pltpu.VMEM((3,) + s, bf16) for s in shards]
+        + [
+            pltpu.VMEM((4, 16, 384), f32), pltpu.VMEM((4, 16, 384), f32), pltpu.VMEM((16, 384), f32),
+            pltpu.VMEM((4, 16, 384), f32), pltpu.VMEM((3, 16, 384), f32),
+            pltpu.VMEM((4, 128, 768), f32), pltpu.VMEM((4, 128, 768), bf16),
+            DMA((2,)), DMA((4, 2)), DMA((4, 2)), DMA((4,)), DMA((4,)), DMA((4, 3)), DMA((4, 3)), DMA((4, 3)), DMA((4, 3)),
+            DMA((8,)), DMA((8,)), DMA((2, 4)), DMA((2, 4)), DMA((2, 3)), DMA((2, 3)),
+        ],
+        compiler_params=pltpu.CompilerParams(collective_id=2, has_side_effects=True, vmem_limit_bytes=VMEM_BYTES),
+        name="reduce",
+    )(gqkv, gout, gup, gdown, gsmall, hout, dxown, dxother)
+
+
+def pad_to(v, rows, columns):
+    return jnp.pad(v, ((0, rows - v.shape[0]), (0, columns - v.shape[1])))
+
+
+def per_slot(hidden_in, lengths, out_grad, w_qkv, qv_bias, w_out, out_biases, norm_gains, norm_biases, w_in, ffn_bias, w_ffo):
+    small_in = jnp.concatenate(
+        [
+            pad_to(jnp.concatenate([out_biases, norm_gains, norm_biases], axis=0), 6, 384),
+            pad_to(qv_bias.reshape(2, 96), 2, 384),
+            ffn_bias.reshape(1, 384),
+            jnp.zeros((7, 384), bf16),
+        ],
+        axis=0,
+    ).astype(f32)
+    xs, ogs, wqkv, wout4, wup, wdown, small = gather(hidden_in, out_grad, w_qkv, w_out, w_in, w_ffo, small_in)
+    xs = xs.reshape(1024, 768)
+    rowp = small[:, 0:6, 0:192].transpose(1, 0, 2).reshape(6, 768)
+    bias = small[:, 6:8, 0:96].reshape(4, 2, 6, 16).transpose(1, 2, 0, 3).reshape(2, 384)
+    upb = small[:, 8, :]
+    q, k, v, mixed, lse = forward(lengths, xs, wqkv, bias)
+    hout, gres, gmixed, gup, gdown, gout, grow, gupb = middle(
+        lengths, mixed, xs, ogs.reshape(512, 768), wout4, wup, wdown, rowp, upb
+    )
+    dxown, dxother, gqkv, gbias = backward(lengths, xs, wqkv, q, k, v, mixed, gmixed, lse, gres)
+    gsmall = jnp.concatenate(
+        [
+            jnp.pad(grow[0:6].reshape(6, 4, 192).transpose(1, 0, 2), ((0, 0), (0, 0), (0, 192))),
+            jnp.pad(gbias[0:2].reshape(2, 6, 4, 16).transpose(2, 0, 1, 3).reshape(4, 2, 96), ((0, 0), (0, 0), (0, 288))),
+            gupb[:, None, :],
+            jnp.zeros((4, 7, 384), f32),
+        ],
+        axis=1,
+    )
+    oqkv, oout, oup, odown, osmall, oh, odx = reduce(
+        gqkv.reshape(3, 4, 192, 384), gout, gup, gdown, gsmall,
+        hout.reshape(4, 128, 768), dxown.reshape(4, 128, 768), dxother.reshape(4, 128, 768),
+    )
+    return (
+        oh,
+        odx,
+        oqkv.astype(f32),
+        osmall[6:8, 0:96].reshape(2, 6, 16),
+        oout.astype(f32),
+        osmall[0:2, 0:192],
+        osmall[2:4, 0:192],
+        osmall[4:6, 0:192],
+        oup.astype(f32),
+        osmall[8],
+        odown.astype(f32),
+    )
+
 
 epsilon = 1e-05
 masked_value = -1e30
@@ -311,8 +1122,9 @@
 
 
 def solution(mesh):
+    one_slot_each = (mesh.shape["fsdp"], mesh.shape["ctx"], mesh.shape["tp"]) == (4, 4, 2)
     return jax.shard_map(
-        per_device,
+        per_slot if one_slot_each else per_device,
         mesh=mesh,
         in_specs=(
             P("fsdp", "ctx", None),

time: 1110 us -> 327 us (0.29)
  waiting for transfers between devices: 729 us -> 0 us
  Pallas kernels: 0 us -> 304 us
  matrix products: 119 us -> 0 us
  blocking collectives: 99.4 us -> 0 us
  local copies, waits for them, and re-layouts: 86.6 us -> 15.2 us
  other arithmetic: 50.7 us -> 6.42 us
  between operations: 15.8 us -> 0.78 us
    all_gather x11 -> x0, waiting for transfers between devices: 315 us -> none  [the longest x4 123 us: attend_slot(): gathered = lax.all_gather(key_value, 'ctx', axis=1, tiled=True)]
    pallas_call x0 -> x5, Pallas kernels: none -> 304 us  [the longest x1 121 us: reduce(): pl.pallas_call(reduce_kernel, out_shape=(struct((3, 192, 384), bf16), str...]
    reduce_scatter x6 -> x0, waiting for transfers between devices: 176 us -> none  [the longest x4 108 us: slot_grads(): lax.psum_scatter(key_terms.astype(jnp.bfloat16), 'ctx', scatter_dimension...]
    unnamed x22 -> x0, waiting for transfers between devices: 125 us -> none
    dot_general x96 -> x0, matrix products: 119 us -> none  [the longest x1 19.5 us: per_device(): jnp.dot(first_low, w_up, preferred_element_type=jnp.float32)]
    psum x5 -> x0, waiting for transfers between devices: 113 us -> none  [the longest x1 70.2 us: per_device(): lax.psum(shares[0].astype(jnp.bfloat16), 'ctx').astype(jnp.float32)]
    all_gather x6 -> x0, blocking collectives: 79.4 us -> none  [the longest x1 24.4 us: per_device(): lax.all_gather(w_out, 'fsdp', axis=1, tiled=True)]
    unnamed x88 -> x22, local copies, waits for them, and re-layouts: 34.5 us -> 6.99 us
  transfers between devices with their start and end apart: 28 -> 0, of which waited for: 27 -> 0; matrix products, arithmetic and copies ran while one was open for 10% -> 0% of each run, Pallas kernels for 0% -> 0%
where the time goes in v1:
time: 327 us; the launch traced here: 326 us
  Pallas kernels  304 us (93%)
  local copies, waits for them, and re-layouts  15.2 us (5%)
  other arithmetic  6.42 us (2%)
    pallas_call x1, Pallas kernels, reduce(): pl.pallas_call(reduce_kernel, out_shape=(struct((3, 192, 384), bf16), str...  121 us
    pallas_call x1, Pallas kernels, gather(): pl.pallas_call(gather_kernel, out_shape=(struct((2, 4, 128, 768), bf16),...  81.2 us
    pallas_call x1, Pallas kernels, middle(): pl.pallas_call(middle_kernel, out_shape=(struct((512, 768), bf16), struct...  48.3 us
    pallas_call x1, Pallas kernels, backward(): pl.pallas_call(backward_kernel, out_shape=(struct((512, 768), f32), struc...  33.3 us
    pallas_call x1, Pallas kernels, forward(): pl.pallas_call(forward_kernel, out_shape=(struct((1024, 384), bf16),) * 4...  20 us
    unnamed x22, local copies, waits for them, and re-layouts  6.99 us

profile of v1, /device:TPU:0, one launch (start us, length us, event | category | flops | bytes accessed | tf_op | source)
XLA Modules:
  0.0 326.3 jit_solution(10312200396615314649)
XLA Ops:
  0.6 1.7 copy.32.out_in
  2.4 0.7 fusion.13
  3.1 0.7 copy.31
  3.8 0.1 reshape.67
  3.9 0.7 reshape.68
  4.6 0.7 fusion.8.small_in
  5.3 81.2 %gather.1 = (bf16[2,4,128,768]{3,2,1,0:T(8,128)(2,1)}, bf16[4,128,768]{2,1,0:T(8,128)(2,1)}, bf16[3,768,384]{2,1,0:T(8,128)(2,1)}, bf16[4,384,192]{2,1,0:T(8,128...) custom-call(bf16[4,256,768]{2,1,0:T(8,128)(2,1)} %x_in.1, ...), custom_call_target="tpu_custom_call" | custom-call | tf_op jit(solution)/shard_map/gather/pallas_call | solution.py:188
  86.5 0.7 slice.30
  87.2 0.1 reshape.70
  87.3 0.7 reshape.71.bias
  88.0 20.0 %attention_forward.1 = (bf16[1024,384]{1,0:T(8,128)(2,1)}, bf16[1024,384]{1,0:T(8,128)(2,1)}, bf16[1024,384]{1,0:T(8,128)(2,1)}, bf16[1024,384]{1,0:T(8,128)(2,1)}, f32[1024,128]{1,0:T(8,128)}) custom-call(s32[4]{0:T(128)} %len_ref.5, bf16[1024,768]{1,0:T(8,128)(2,1)} %bitcast.18, bf16[3,768,384]{2,1,0:T(8,128)(2,1)} %get-tuple-element.43.wqkv, ...), custom_call_target="tpu_custom_call" | custom-call | tf_op jit(solution)/shard_map/attention_forward/pallas_call | solution.py:339
  108.0 0.6 slice_bitcast_fusion.1.upb
  108.6 0.7 reshape.73.rowp
  109.3 48.3 %rows.1 = (bf16[512,768]{1,0:T(8,128)(2,1)}, f32[512,768]{1,0:T(8,128)}, bf16[1024,384]{1,0:T(8,128)(2,1)}, bf16[4,768,384]{2,1,0:T(8,128)(2,1)}, bf16[4,384,768...) custom-call(s32[4]{0:T(128)} %len_ref.5, ...), custom_call_target="tpu_custom_call" | custom-call | tf_op jit(solution)/shard_map/rows/pallas_call | solution.py:598
  157.6 33.3 %attention_backward.1 = (f32[512,768]{1,0:T(8,128)}, f32[512,768]{1,0:T(8,128)}, bf16[3,768,384]{2,1,0:T(8,128)(2,1)}, f32[8,384]{1,0:T(8,128)}) custom-call(s32[4]{0:T(128)} %len_ref.5, bf16[1024,768]{1,0:T(8,128)(2,1)} %bitcast.20, bf16[3,768,384]{2,1,0:T(8,128)(2,1)} %get-tuple-element.43.wqkv, bf16[1024,384]{1,0:T(8,128)(2,1)} %get-tuple-element.45.q_ref, ...), custom_call_target="tpu_custom_call" | custom-call | tf_op jit(solution)/shard_map/attention_backward/pallas_call | solution.py:389
  191.0 0.7 slice.34
  191.7 0.1 reshape.76
  191.8 0.1 reshape.77
  191.9 0.1 reshape.75
  192.1 0.7 fusion.1.gsmall
  192.8 121.2 %reduce.3 = (bf16[3,192,384]{2,1,0:T(8,128)(2,1)}, bf16[384,192]{1,0:T(8,128)(2,1)}, bf16[768,384]{1,0:T(8,128)(2,1)}, bf16[384,768]{1,0:T(8,128)(2,1)}, f32[16,...) custom-call(bf16[3,4,192,384]{3,2,1,0:T(8,128)(2,1)} %bitcast.21, ...), custom_call_target="tpu_custom_call" | custom-call | tf_op jit(solution)/shard_map/reduce/pallas_call | solution.py:738
  314.0 2.2 convert_element_type.26
  316.2 1.1 convert_element_type.27
  317.3 1.0 convert_element_type.24
  318.3 0.8 copy.39
  319.1 0.7 slice.35
  319.9 0.6 copy.38
  320.5 1.4 fusion.14
  321.9 1.3 slice_reduce_fusion
  323.2 1.1 copy.46
  324.3 0.8 copy-done
  325.2 1.1 copy.47
  (27 shorter events, 0.4 us)
Async XLA Ops:
  88.0 20.0 %copy-start.5 = (f32[4,16,384]{2,1,0:T(8,128)S(1)}, f32[4,16,384]{2,1,0:T(8,128)}, u32[]{:S(2)}) copy-start(f32[4,16,384]{2,1,0:T(8,128)} %get-tuple-element.44) | copy-start | bytes 294916
  157.6 34.2 %copy-start.6 = (f32[8,768]{1,0:T(8,128)S(1)}, f32[8,768]{1,0:T(8,128)}, u32[]{:S(2)}) copy-start(f32[8,768]{1,0:T(8,128)} %get-tuple-element.60) | copy-start | bytes 73732
  157.6 34.3 %copy-start.7 = (f32[4,384]{1,0:T(4,128)S(1)}, f32[4,384]{1,0:T(4,128)}, u32[]{:S(2)}) copy-start(f32[4,384]{1,0:T(4,128)} %get-tuple-element.62) | copy-start | bytes 18436
  314.0 2.3 copy-start.2
  314.0 3.3 %copy-start.3 = (bf16[3,192,384]{2,1,0:T(8,128)(2,1)S(1)}, bf16[3,192,384]{2,1,0:T(8,128)(2,1)}, u32[]{:S(2)}) copy-start(bf16[3,192,384]{2,1,0:T(8,128)(2,1)} %get-tuple-element.68) | copy-start | bytes 1327108
  316.2 2.1 copy-start.4
  316.2 7.0 %copy-start.1 = (bf16[4,256,768]{2,1,0:T(8,128)(2,1)S(1)}, bf16[4,256,768]{2,1,0:T(8,128)(2,1)}, u32[]{:S(2)}) copy-start(bf16[4,256,768]{2,1,0:T(8,128)(2,1)} %get-tuple-element.109) | copy-start | bytes 4718596
  323.2 2.0 copy-start
